TPU v7x, 512 devices: a whole 4x8x8 slice. The times are simulated.
512 devices in a mesh: cuts: 8 (over y), row: 64 (over x, z, core).
Axes of the slice: x: 4, y: 8, z: 8, core: 2. Of those that a mesh axis runs over, the one named last changes fastest.
Arguments:
- block_tiles: float32 [192, 24, 128, 128], P('row'), may hold values from -0.109375 to 0.109375
- tile_pattern: int32 [192, 24], P('row'), may hold values from 0 to 191, as said below
- start_vectors: float32 [8, 32, 24576], P('cuts', None, 'row'), may hold values from -8 to 8
- centers: float32 [8], P('cuts'), may hold values from -0.3 to 0.3
- halfwidths: float32 [8], P('cuts'), may hold values from 0.9 to 1.3
- dup_pairs: int32 [8, 8, 2], P('cuts'), may hold values from 0 to 31, as said below
Outputs:
- filtered_basis: float32 [8, 32, 24576], P('cuts', None, 'row')
- projected: float32 [8, 32, 32], P('cuts')
Inputs may be any that keep to these rules, and one draw needn't show every extreme that they name: tile_pattern[r, 0] = r; the other entries of block row r are distinct block rows, each within 12 of r cyclically and different from r. `dup_pairs`: within one slice the first entries of the pairs are distinct, and so are the second entries; the pairs of slice 0 are not used.
All inputs are finite; a program needn't handle non-finite values.
Results may differ from a plain program's by a relative error of at most 0.00015.
Values sent between devices are 32-bit elements; how exact they have to be, the bound alone decides.
A program may use at most 64 MiB of HBM per device.

v0:
```python
import math
import jax
import jax.numpy as jnp
from jax import lax
from jax.sharding import PartitionSpec as P

DEG = 8
REACH = 12


def from_behind(shard, axis, by):
    size = lax.axis_size(axis)
    return lax.ppermute(shard, axis, [(i, (i + by) % size) for i in range(size)])


def from_behind_2(value, axis, steps):
    count = lax.axis_size(axis)
    leading, last = (max(0, -steps), min(count, count - steps))
    return lax.ppermute(value, axis, [(source, source + steps) for source in range(leading, last)])


def apply_local(vectors, block_tiles, tile_pattern):
    vec_count = vectors.shape[0]
    local_rows = block_tiles.shape[0]
    tile_width = block_tiles.shape[2]
    device_reach = (REACH + local_rows - 1) // local_rows
    pieces = []
    for offset in range(-device_reach, device_reach + 1):
        if offset == 0:
            pieces.append(vectors)
        else:
            pieces.append(from_behind(vectors, "row", -offset))
    extended = jnp.concatenate(pieces, axis=1).reshape(
        vec_count, len(pieces) * local_rows, tile_width
    )
    total_rows = local_rows * lax.axis_size("row")
    lowest = (lax.axis_index("row") - device_reach) * local_rows
    positions = (tile_pattern - lowest) % total_rows
    picked = jnp.take(extended, positions, axis=1)
    product = jnp.einsum("vrkc,rkdc->vrd", picked, block_tiles, precision=lax.Precision.HIGHEST)
    return product.reshape(vec_count, local_rows * tile_width)


def lower_solve(factor, right_side):
    return lax.linalg.triangular_solve(factor, right_side, left_side=True, lower=True)


def local(block_tiles, tile_pattern, start_vectors, centers, halfwidths, dup_pairs):
    initial = start_vectors[0]
    center = centers[0]
    halfwidth = halfwidths[0]
    order_total = initial.shape[1] * lax.axis_size("row")
    previous = initial
    current = (apply_local(initial, block_tiles, tile_pattern) - center * initial) / halfwidth
    for degree in range(DEG - 1):
        following = (
            2.0 * (apply_local(current, block_tiles, tile_pattern) - center * current) / halfwidth
            - previous
        )
        previous, current = (current, following)
    gram_matrix = lax.psum(jnp.dot(current, current.T, precision=lax.Precision.HIGHEST), "row")
    factor = jnp.linalg.cholesky(gram_matrix)
    basis_raw = math.sqrt(order_total) * lower_solve(factor, current)
    imaged = apply_local(basis_raw, block_tiles, tile_pattern)
    projected = (
        lax.psum(jnp.dot(basis_raw, imaged.T, precision=lax.Precision.HIGHEST), "row") / order_total
    )
    vec_count = basis_raw.shape[0]
    columns = jnp.arange(vec_count, dtype=jnp.int32)
    own_index = dup_pairs[0, :, 0]
    their_index = dup_pairs[0, :, 1]
    target_mask = (own_index[:, None] == columns[None, :]).astype(jnp.float32)
    lower_basis = from_behind_2(basis_raw, "cuts", 1)
    selector = (their_index[:, None] == columns[None, :]).astype(jnp.float32)
    lower_rows = jnp.dot(selector, lower_basis, precision=lax.Precision.HIGHEST)
    correlation = (
        lax.psum(jnp.dot(lower_rows, basis_raw.T, precision=lax.Precision.HIGHEST), "row")
        / order_total
    )
    filtered_basis = basis_raw - jnp.dot(
        (target_mask * correlation).T, lower_rows, precision=lax.Precision.HIGHEST
    )
    return (filtered_basis[None], projected[None])


def solution(mesh):
    in_specs = (
        P("row", None, None, None),
        P("row", None),
        P("cuts", None, "row"),
        P("cuts"),
        P("cuts"),
        P("cuts", None, None),
    )
    out_specs = (P("cuts", None, "row"), P("cuts", None, None))
    return jax.shard_map(local, mesh=mesh, in_specs=in_specs, out_specs=out_specs, check_vma=False)
```

profile of v0, /device:TPU:32, one launch (start us, length us, event | category | flops | bytes accessed | tf_op | source)
XLA Modules:
  0.0 861.8 jit_solution(17012417078433444619)
XLA Ops:
  0.6 6.1 collective-permute-start
  6.7 3.4 collective-permute-start.1
  10.2 5.5 collective-permute-start.2
  15.7 3.5 collective-permute-start.3
  19.2 5.4 collective-permute-start.4
  31.8 5.5 collective-permute-start.7
  40.6 6.7 fusion.16
  47.3 4.9 collective-permute-start.8
  58.4 6.5 collective-permute-start.12
  65.0 3.9 collective-permute-start.13
  71.7 3.7 collective-permute-start.15
  75.6 3.8 collective-permute-done.15
  80.1 6.7 fusion.14
  96.0 6.7 collective-permute-start.20
  102.8 3.5 collective-permute-start.21
  106.3 2.8 collective-permute-start.22
  109.2 5.1 collective-permute-start.23
  114.4 3.0 collective-permute-done.23
  118.2 6.7 fusion.12
  133.3 6.8 collective-permute-start.28
  140.1 3.9 collective-permute-start.29
  146.8 5.6 collective-permute-start.31
  155.4 6.7 fusion.10
  171.2 6.6 collective-permute-start.36
  177.8 3.6 collective-permute-start.37
  181.4 2.8 collective-permute-start.38
  184.3 6.1 collective-permute-start.39
  193.2 6.7 fusion.8
  208.7 6.6 collective-permute-start.44
  215.3 3.7 collective-permute-start.45
  221.9 6.0 collective-permute-start.47
  230.7 6.7 fusion.6
  246.5 6.6 collective-permute-start.52
  253.1 3.5 collective-permute-start.53
  259.5 6.0 collective-permute-start.55
  268.5 6.7 fusion.4
  284.1 6.6 collective-permute-start.60
  290.7 3.6 collective-permute-start.61
  297.1 6.0 collective-permute-start.63
  306.1 7.2 fusion.43
  313.5 250.9 %psum.21 = f32[32,32]{0,1:T(8,128)S(1)} all-reduce(f32[32,32]{0,1:T(8,128)S(1)} %convolution_bitcast_fusion), channel_id=1, replica_groups=mesh['cuts'=8,'row'=64] {'row'}, use_global_device_ids=true, to_apply=%region_0.2 | all-reduce | flops 1024 | bytes 8192 | tf_op jit(solution)/shard_map/psum | solution.py:61
  564.5 2.9 cholesky.16
  579.2 7.0 collective-permute-start.69
  586.2 3.9 collective-permute-start.70
  590.1 2.9 collective-permute-start.71
  593.1 5.9 collective-permute-start.72
  602.4 6.7 fusion.30
  609.7 250.6 %all-reduce = (f32[8,32]{1,0:T(8,128)S(1)}, f32[32,32]{1,0:T(8,128)S(1)}) all-reduce(f32[8,32]{1,0:T(8,128)S(1)} %fusion.129, f32[32,32]{1,0:T(8,128)S(1)} %fusion.64), channel_id=1, replica_groups=mesh['cuts'=8,'row'=64] {'row'}, use_global_device_ids=true, to_apply=%region_3.5 | all-reduce | flops 1280 | bytes 10240 | tf_op jit(solution)/shard_map/psum | solution.py:77
  (237 shorter events, 115.5 us)
Async XLA Ops:
  0.6 26.9 %collective-permute-start = (f32[32,384]{1,0:T(8,128)}, f32[32,384]{1,0:T(8,128)S(1)}, u32[]{:S(2)}, u32[]{:S(2)}) collective-permute-start(f32[32,384]{1,0:T(8,128)} %bitcast.384), channel_id=1, source_target_pairs={{0,4},{1,5},{2,6},{3,7},{4,8},{5,9},{6,10},{7,11},{8,12},{9,13},{1... | collective-permute-start | bytes 147464 | tf_op jit(solution)/shard_map/ppermute | solution.py:13
  6.7 23.1 %collective-permute-start.1 = (f32[32,384]{1,0:T(8,128)}, f32[32,384]{1,0:T(8,128)S(1)}, u32[]{:S(2)}, u32[]{:S(2)}) collective-permute-start(f32[32,384]{1,0:T(8,128)} %bitcast.385), channel_id=1, source_target_pairs={{0,3},{1,4},{2,5},{3,6},{4,7},{5,8},{6,9},{7,10},{8,11},{9,12},{10... | collective-permute-start | bytes 147464 | tf_op jit(solution)/shard_map/ppermute | solution.py:13
  10.2 21.6 %collective-permute-start.2 = (f32[32,384]{1,0:T(8,128)}, f32[32,384]{1,0:T(8,128)S(1)}, u32[]{:S(2)}, u32[]{:S(2)}) collective-permute-start(f32[32,384]{1,0:T(8,128)} %bitcast.386), channel_id=1, source_target_pairs={{0,2},{1,3},{2,4},{3,5},{4,6},{5,7},{6,8},{7,9},{8,10},{9,11},{10,... | collective-permute-start | bytes 147464 | tf_op jit(solution)/shard_map/ppermute | solution.py:13
  15.7 21.6 %collective-permute-start.3 = (f32[32,384]{1,0:T(8,128)}, f32[32,384]{1,0:T(8,128)S(1)}, u32[]{:S(2)}, u32[]{:S(2)}) collective-permute-start(f32[32,384]{1,0:T(8,128)} %bitcast.387), channel_id=1, source_target_pairs={{0,1},{1,2},{2,3},{3,4},{4,5},{5,6},{6,7},{7,8},{8,9},{9,10},{10,1... | collective-permute-start | bytes 147464 | tf_op jit(solution)/shard_map/ppermute | solution.py:13
  19.2 18.1 %collective-permute-start.4 = (f32[32,384]{1,0:T(8,128)}, f32[32,384]{1,0:T(8,128)S(1)}, u32[]{:S(2)}, u32[]{:S(2)}) collective-permute-start(f32[32,384]{1,0:T(8,128)} %bitcast.388), channel_id=1, source_target_pairs={{0,63},{1,0},{2,1},{3,2},{4,3},{5,4},{6,5},{7,6},{8,7},{9,8},{10,9... | collective-permute-start | bytes 147464 | tf_op jit(solution)/shard_map/ppermute | solution.py:13
  47.3 17.7 %collective-permute-start.8 = (f32[32,384]{1,0:T(8,128)S(1)}, f32[32,384]{1,0:T(8,128)S(1)}, u32[]{:S(2)}, u32[]{:S(2)}) collective-permute-start(f32[32,384]{1,0:T(8,128)S(1)} %fusion.87), channel_id=1, source_target_pairs={{0,4},{1,5},{2,6},{3,7},{4,8},{5,9},{6,10},{7,11},{8,12},{9,13},{1... | collective-permute-start | bytes 147464 | tf_op jit(solution)/shard_map/ppermute | solution.py:13
  52.2 16.7 %collective-permute-start.9 = (f32[32,384]{1,0:T(8,128)S(1)}, f32[32,384]{1,0:T(8,128)S(1)}, u32[]{:S(2)}, u32[]{:S(2)}) collective-permute-start(f32[32,384]{1,0:T(8,128)S(1)} %fusion.87), channel_id=1, source_target_pairs={{0,3},{1,4},{2,5},{3,6},{4,7},{5,8},{6,9},{7,10},{8,11},{9,12},{10... | collective-permute-start | bytes 147464 | tf_op jit(solution)/shard_map/ppermute | solution.py:13
  54.1 17.6 %collective-permute-start.10 = (f32[32,384]{1,0:T(8,128)S(1)}, f32[32,384]{1,0:T(8,128)S(1)}, u32[]{:S(2)}, u32[]{:S(2)}) collective-permute-start(f32[32,384]{1,0:T(8,128)S(1)} %fusion.87), channel_id=1, source_target_pairs={{0,2},{1,3},{2,4},{3,5},{4,6},{5,7},{6,8},{7,9},{8,10},{9,11},{10,... | collective-permute-start | bytes 147464 | tf_op jit(solution)/shard_map/ppermute | solution.py:13
  56.1 19.4 %collective-permute-start.11 = (f32[32,384]{1,0:T(8,128)S(1)}, f32[32,384]{1,0:T(8,128)S(1)}, u32[]{:S(2)}, u32[]{:S(2)}) collective-permute-start(f32[32,384]{1,0:T(8,128)S(1)} %fusion.87), channel_id=1, source_target_pairs={{0,1},{1,2},{2,3},{3,4},{4,5},{5,6},{6,7},{7,8},{8,9},{9,10},{10,1... | collective-permute-start | bytes 147464 | tf_op jit(solution)/shard_map/ppermute | solution.py:13
  58.4 17.1 %collective-permute-start.12 = (f32[32,384]{1,0:T(8,128)S(1)}, f32[32,384]{1,0:T(8,128)S(1)}, u32[]{:S(2)}, u32[]{:S(2)}) collective-permute-start(f32[32,384]{1,0:T(8,128)S(1)} %fusion.87), channel_id=1, source_target_pairs={{0,63},{1,0},{2,1},{3,2},{4,3},{5,4},{6,5},{7,6},{8,7},{9,8},{10,9... | collective-permute-start | bytes 147464 | tf_op jit(solution)/shard_map/ppermute | solution.py:13
  86.8 15.9 %collective-permute-start.16 = (f32[32,384]{1,0:T(8,128)S(1)}, f32[32,384]{1,0:T(8,128)S(1)}, u32[]{:S(2)}, u32[]{:S(2)}) collective-permute-start(f32[32,384]{1,0:T(8,128)S(1)} %fusion.86), channel_id=1, source_target_pairs={{0,4},{1,5},{2,6},{3,7},{4,8},{5,9},{6,10},{7,11},{8,12},{9,13},{1... | collective-permute-start | bytes 147464 | tf_op jit(solution)/shard_map/ppermute | solution.py:13
  89.6 16.7 %collective-permute-start.17 = (f32[32,384]{1,0:T(8,128)S(1)}, f32[32,384]{1,0:T(8,128)S(1)}, u32[]{:S(2)}, u32[]{:S(2)}) collective-permute-start(f32[32,384]{1,0:T(8,128)S(1)} %fusion.86), channel_id=1, source_target_pairs={{0,3},{1,4},{2,5},{3,6},{4,7},{5,8},{6,9},{7,10},{8,11},{9,12},{10... | collective-permute-start | bytes 147464 | tf_op jit(solution)/shard_map/ppermute | solution.py:13
  91.5 17.6 %collective-permute-start.18 = (f32[32,384]{1,0:T(8,128)S(1)}, f32[32,384]{1,0:T(8,128)S(1)}, u32[]{:S(2)}, u32[]{:S(2)}) collective-permute-start(f32[32,384]{1,0:T(8,128)S(1)} %fusion.86), channel_id=1, source_target_pairs={{0,2},{1,3},{2,4},{3,5},{4,6},{5,7},{6,8},{7,9},{8,10},{9,11},{10,... | collective-permute-start | bytes 147464 | tf_op jit(solution)/shard_map/ppermute | solution.py:13
  93.9 20.5 %collective-permute-start.19 = (f32[32,384]{1,0:T(8,128)S(1)}, f32[32,384]{1,0:T(8,128)S(1)}, u32[]{:S(2)}, u32[]{:S(2)}) collective-permute-start(f32[32,384]{1,0:T(8,128)S(1)} %fusion.86), channel_id=1, source_target_pairs={{0,1},{1,2},{2,3},{3,4},{4,5},{5,6},{6,7},{7,8},{8,9},{9,10},{10,1... | collective-permute-start | bytes 147464 | tf_op jit(solution)/shard_map/ppermute | solution.py:13
  96.0 18.3 %collective-permute-start.20 = (f32[32,384]{1,0:T(8,128)S(1)}, f32[32,384]{1,0:T(8,128)S(1)}, u32[]{:S(2)}, u32[]{:S(2)}) collective-permute-start(f32[32,384]{1,0:T(8,128)S(1)} %fusion.86), channel_id=1, source_target_pairs={{0,63},{1,0},{2,1},{3,2},{4,3},{5,4},{6,5},{7,6},{8,7},{9,8},{10,9... | collective-permute-start | bytes 147464 | tf_op jit(solution)/shard_map/ppermute | solution.py:13
  124.9 15.1 %collective-permute-start.24 = (f32[32,384]{1,0:T(8,128)S(1)}, f32[32,384]{1,0:T(8,128)S(1)}, u32[]{:S(2)}, u32[]{:S(2)}) collective-permute-start(f32[32,384]{1,0:T(8,128)S(1)} %fusion.83), channel_id=1, source_target_pairs={{0,4},{1,5},{2,6},{3,7},{4,8},{5,9},{6,10},{7,11},{8,12},{9,13},{1... | collective-permute-start | bytes 147464 | tf_op jit(solution)/shard_map/ppermute | solution.py:13
  127.3 16.7 %collective-permute-start.25 = (f32[32,384]{1,0:T(8,128)S(1)}, f32[32,384]{1,0:T(8,128)S(1)}, u32[]{:S(2)}, u32[]{:S(2)}) collective-permute-start(f32[32,384]{1,0:T(8,128)S(1)} %fusion.83), channel_id=1, source_target_pairs={{0,3},{1,4},{2,5},{3,6},{4,7},{5,8},{6,9},{7,10},{8,11},{9,12},{10... | collective-permute-start | bytes 147464 | tf_op jit(solution)/shard_map/ppermute | solution.py:13
  129.2 17.6 %collective-permute-start.26 = (f32[32,384]{1,0:T(8,128)S(1)}, f32[32,384]{1,0:T(8,128)S(1)}, u32[]{:S(2)}, u32[]{:S(2)}) collective-permute-start(f32[32,384]{1,0:T(8,128)S(1)} %fusion.83), channel_id=1, source_target_pairs={{0,2},{1,3},{2,4},{3,5},{4,6},{5,7},{6,8},{7,9},{8,10},{9,11},{10,... | collective-permute-start | bytes 147464 | tf_op jit(solution)/shard_map/ppermute | solution.py:13
  131.1 21.2 %collective-permute-start.27 = (f32[32,384]{1,0:T(8,128)S(1)}, f32[32,384]{1,0:T(8,128)S(1)}, u32[]{:S(2)}, u32[]{:S(2)}) collective-permute-start(f32[32,384]{1,0:T(8,128)S(1)} %fusion.83), channel_id=1, source_target_pairs={{0,1},{1,2},{2,3},{3,4},{4,5},{5,6},{6,7},{7,8},{8,9},{9,10},{10,1... | collective-permute-start | bytes 147464 | tf_op jit(solution)/shard_map/ppermute | solution.py:13
  133.3 19.2 %collective-permute-start.28 = (f32[32,384]{1,0:T(8,128)S(1)}, f32[32,384]{1,0:T(8,128)S(1)}, u32[]{:S(2)}, u32[]{:S(2)}) collective-permute-start(f32[32,384]{1,0:T(8,128)S(1)} %fusion.83), channel_id=1, source_target_pairs={{0,63},{1,0},{2,1},{3,2},{4,3},{5,4},{6,5},{7,6},{8,7},{9,8},{10,9... | collective-permute-start | bytes 147464 | tf_op jit(solution)/shard_map/ppermute | solution.py:13
  162.1 15.7 %collective-permute-start.32 = (f32[32,384]{1,0:T(8,128)S(1)}, f32[32,384]{1,0:T(8,128)S(1)}, u32[]{:S(2)}, u32[]{:S(2)}) collective-permute-start(f32[32,384]{1,0:T(8,128)S(1)} %fusion.80), channel_id=1, source_target_pairs={{0,4},{1,5},{2,6},{3,7},{4,8},{5,9},{6,10},{7,11},{8,12},{9,13},{1... | collective-permute-start | bytes 147464 | tf_op jit(solution)/shard_map/ppermute | solution.py:13
  164.7 16.7 %collective-permute-start.33 = (f32[32,384]{1,0:T(8,128)S(1)}, f32[32,384]{1,0:T(8,128)S(1)}, u32[]{:S(2)}, u32[]{:S(2)}) collective-permute-start(f32[32,384]{1,0:T(8,128)S(1)} %fusion.80), channel_id=1, source_target_pairs={{0,3},{1,4},{2,5},{3,6},{4,7},{5,8},{6,9},{7,10},{8,11},{9,12},{10... | collective-permute-start | bytes 147464 | tf_op jit(solution)/shard_map/ppermute | solution.py:13
  166.6 17.6 %collective-permute-start.34 = (f32[32,384]{1,0:T(8,128)S(1)}, f32[32,384]{1,0:T(8,128)S(1)}, u32[]{:S(2)}, u32[]{:S(2)}) collective-permute-start(f32[32,384]{1,0:T(8,128)S(1)} %fusion.80), channel_id=1, source_target_pairs={{0,2},{1,3},{2,4},{3,5},{4,6},{5,7},{6,8},{7,9},{8,10},{9,11},{10,... | collective-permute-start | bytes 147464 | tf_op jit(solution)/shard_map/ppermute | solution.py:13
  168.8 21.6 %collective-permute-start.35 = (f32[32,384]{1,0:T(8,128)S(1)}, f32[32,384]{1,0:T(8,128)S(1)}, u32[]{:S(2)}, u32[]{:S(2)}) collective-permute-start(f32[32,384]{1,0:T(8,128)S(1)} %fusion.80), channel_id=1, source_target_pairs={{0,1},{1,2},{2,3},{3,4},{4,5},{5,6},{6,7},{7,8},{8,9},{9,10},{10,1... | collective-permute-start | bytes 147464 | tf_op jit(solution)/shard_map/ppermute | solution.py:13
  171.2 19.2 %collective-permute-start.36 = (f32[32,384]{1,0:T(8,128)S(1)}, f32[32,384]{1,0:T(8,128)S(1)}, u32[]{:S(2)}, u32[]{:S(2)}) collective-permute-start(f32[32,384]{1,0:T(8,128)S(1)} %fusion.80), channel_id=1, source_target_pairs={{0,63},{1,0},{2,1},{3,2},{4,3},{5,4},{6,5},{7,6},{8,7},{9,8},{10,9... | collective-permute-start | bytes 147464 | tf_op jit(solution)/shard_map/ppermute | solution.py:13
  177.8 12.7 %collective-permute-start.37 = (f32[32,384]{1,0:T(8,128)S(1)}, f32[32,384]{1,0:T(8,128)S(1)}, u32[]{:S(2)}, u32[]{:S(2)}) collective-permute-start(f32[32,384]{1,0:T(8,128)S(1)} %fusion.80), channel_id=1, source_target_pairs={{0,62},{1,63},{2,0},{3,1},{4,2},{5,3},{6,4},{7,5},{8,6},{9,7},{10,... | collective-permute-start | bytes 147464 | tf_op jit(solution)/shard_map/ppermute | solution.py:13
  200.0 15.3 %collective-permute-start.40 = (f32[32,384]{1,0:T(8,128)S(1)}, f32[32,384]{1,0:T(8,128)S(1)}, u32[]{:S(2)}, u32[]{:S(2)}) collective-permute-start(f32[32,384]{1,0:T(8,128)S(1)} %fusion.77), channel_id=1, source_target_pairs={{0,4},{1,5},{2,6},{3,7},{4,8},{5,9},{6,10},{7,11},{8,12},{9,13},{1... | collective-permute-start | bytes 147464 | tf_op jit(solution)/shard_map/ppermute | solution.py:13
  202.3 16.7 %collective-permute-start.41 = (f32[32,384]{1,0:T(8,128)S(1)}, f32[32,384]{1,0:T(8,128)S(1)}, u32[]{:S(2)}, u32[]{:S(2)}) collective-permute-start(f32[32,384]{1,0:T(8,128)S(1)} %fusion.77), channel_id=1, source_target_pairs={{0,3},{1,4},{2,5},{3,6},{4,7},{5,8},{6,9},{7,10},{8,11},{9,12},{10... | collective-permute-start | bytes 147464 | tf_op jit(solution)/shard_map/ppermute | solution.py:13
  204.3 17.6 %collective-permute-start.42 = (f32[32,384]{1,0:T(8,128)S(1)}, f32[32,384]{1,0:T(8,128)S(1)}, u32[]{:S(2)}, u32[]{:S(2)}) collective-permute-start(f32[32,384]{1,0:T(8,128)S(1)} %fusion.77), channel_id=1, source_target_pairs={{0,2},{1,3},{2,4},{3,5},{4,6},{5,7},{6,8},{7,9},{8,10},{9,11},{10,... | collective-permute-start | bytes 147464 | tf_op jit(solution)/shard_map/ppermute | solution.py:13
  206.2 21.7 %collective-permute-start.43 = (f32[32,384]{1,0:T(8,128)S(1)}, f32[32,384]{1,0:T(8,128)S(1)}, u32[]{:S(2)}, u32[]{:S(2)}) collective-permute-start(f32[32,384]{1,0:T(8,128)S(1)} %fusion.77), channel_id=1, source_target_pairs={{0,1},{1,2},{2,3},{3,4},{4,5},{5,6},{6,7},{7,8},{8,9},{9,10},{10,1... | collective-permute-start | bytes 147464 | tf_op jit(solution)/shard_map/ppermute | solution.py:13
  208.7 19.2 %collective-permute-start.44 = (f32[32,384]{1,0:T(8,128)S(1)}, f32[32,384]{1,0:T(8,128)S(1)}, u32[]{:S(2)}, u32[]{:S(2)}) collective-permute-start(f32[32,384]{1,0:T(8,128)S(1)} %fusion.77), channel_id=1, source_target_pairs={{0,63},{1,0},{2,1},{3,2},{4,3},{5,4},{6,5},{7,6},{8,7},{9,8},{10,9... | collective-permute-start | bytes 147464 | tf_op jit(solution)/shard_map/ppermute | solution.py:13
  215.3 12.7 %collective-permute-start.45 = (f32[32,384]{1,0:T(8,128)S(1)}, f32[32,384]{1,0:T(8,128)S(1)}, u32[]{:S(2)}, u32[]{:S(2)}) collective-permute-start(f32[32,384]{1,0:T(8,128)S(1)} %fusion.77), channel_id=1, source_target_pairs={{0,62},{1,63},{2,0},{3,1},{4,2},{5,3},{6,4},{7,5},{8,6},{9,7},{10,... | collective-permute-start | bytes 147464 | tf_op jit(solution)/shard_map/ppermute | solution.py:13
  237.4 15.6 %collective-permute-start.48 = (f32[32,384]{1,0:T(8,128)S(1)}, f32[32,384]{1,0:T(8,128)S(1)}, u32[]{:S(2)}, u32[]{:S(2)}) collective-permute-start(f32[32,384]{1,0:T(8,128)S(1)} %fusion.74), channel_id=1, source_target_pairs={{0,4},{1,5},{2,6},{3,7},{4,8},{5,9},{6,10},{7,11},{8,12},{9,13},{1... | collective-permute-start | bytes 147464 | tf_op jit(solution)/shard_map/ppermute | solution.py:13
  239.9 16.7 %collective-permute-start.49 = (f32[32,384]{1,0:T(8,128)S(1)}, f32[32,384]{1,0:T(8,128)S(1)}, u32[]{:S(2)}, u32[]{:S(2)}) collective-permute-start(f32[32,384]{1,0:T(8,128)S(1)} %fusion.74), channel_id=1, source_target_pairs={{0,3},{1,4},{2,5},{3,6},{4,7},{5,8},{6,9},{7,10},{8,11},{9,12},{10... | collective-permute-start | bytes 147464 | tf_op jit(solution)/shard_map/ppermute | solution.py:13
  241.9 17.6 %collective-permute-start.50 = (f32[32,384]{1,0:T(8,128)S(1)}, f32[32,384]{1,0:T(8,128)S(1)}, u32[]{:S(2)}, u32[]{:S(2)}) collective-permute-start(f32[32,384]{1,0:T(8,128)S(1)} %fusion.74), channel_id=1, source_target_pairs={{0,2},{1,3},{2,4},{3,5},{4,6},{5,7},{6,8},{7,9},{8,10},{9,11},{10,... | collective-permute-start | bytes 147464 | tf_op jit(solution)/shard_map/ppermute | solution.py:13
  244.2 21.4 %collective-permute-start.51 = (f32[32,384]{1,0:T(8,128)S(1)}, f32[32,384]{1,0:T(8,128)S(1)}, u32[]{:S(2)}, u32[]{:S(2)}) collective-permute-start(f32[32,384]{1,0:T(8,128)S(1)} %fusion.74), channel_id=1, source_target_pairs={{0,1},{1,2},{2,3},{3,4},{4,5},{5,6},{6,7},{7,8},{8,9},{9,10},{10,1... | collective-permute-start | bytes 147464 | tf_op jit(solution)/shard_map/ppermute | solution.py:13
  246.5 19.1 %collective-permute-start.52 = (f32[32,384]{1,0:T(8,128)S(1)}, f32[32,384]{1,0:T(8,128)S(1)}, u32[]{:S(2)}, u32[]{:S(2)}) collective-permute-start(f32[32,384]{1,0:T(8,128)S(1)} %fusion.74), channel_id=1, source_target_pairs={{0,63},{1,0},{2,1},{3,2},{4,3},{5,4},{6,5},{7,6},{8,7},{9,8},{10,9... | collective-permute-start | bytes 147464 | tf_op jit(solution)/shard_map/ppermute | solution.py:13
  275.2 15.4 %collective-permute-start.56 = (f32[32,384]{1,0:T(8,128)S(1)}, f32[32,384]{1,0:T(8,128)S(1)}, u32[]{:S(2)}, u32[]{:S(2)}) collective-permute-start(f32[32,384]{1,0:T(8,128)S(1)} %fusion.71), channel_id=1, source_target_pairs={{0,4},{1,5},{2,6},{3,7},{4,8},{5,9},{6,10},{7,11},{8,12},{9,13},{1... | collective-permute-start | bytes 147464 | tf_op jit(solution)/shard_map/ppermute | solution.py:13
  277.6 16.7 %collective-permute-start.57 = (f32[32,384]{1,0:T(8,128)S(1)}, f32[32,384]{1,0:T(8,128)S(1)}, u32[]{:S(2)}, u32[]{:S(2)}) collective-permute-start(f32[32,384]{1,0:T(8,128)S(1)} %fusion.71), channel_id=1, source_target_pairs={{0,3},{1,4},{2,5},{3,6},{4,7},{5,8},{6,9},{7,10},{8,11},{9,12},{10... | collective-permute-start | bytes 147464 | tf_op jit(solution)/shard_map/ppermute | solution.py:13
  279.5 17.6 %collective-permute-start.58 = (f32[32,384]{1,0:T(8,128)S(1)}, f32[32,384]{1,0:T(8,128)S(1)}, u32[]{:S(2)}, u32[]{:S(2)}) collective-permute-start(f32[32,384]{1,0:T(8,128)S(1)} %fusion.71), channel_id=1, source_target_pairs={{0,2},{1,3},{2,4},{3,5},{4,6},{5,7},{6,8},{7,9},{8,10},{9,11},{10,... | collective-permute-start | bytes 147464 | tf_op jit(solution)/shard_map/ppermute | solution.py:13
  281.7 21.5 %collective-permute-start.59 = (f32[32,384]{1,0:T(8,128)S(1)}, f32[32,384]{1,0:T(8,128)S(1)}, u32[]{:S(2)}, u32[]{:S(2)}) collective-permute-start(f32[32,384]{1,0:T(8,128)S(1)} %fusion.71), channel_id=1, source_target_pairs={{0,1},{1,2},{2,3},{3,4},{4,5},{5,6},{6,7},{7,8},{8,9},{9,10},{10,1... | collective-permute-start | bytes 147464 | tf_op jit(solution)/shard_map/ppermute | solution.py:13
  284.1 19.1 %collective-permute-start.60 = (f32[32,384]{1,0:T(8,128)S(1)}, f32[32,384]{1,0:T(8,128)S(1)}, u32[]{:S(2)}, u32[]{:S(2)}) collective-permute-start(f32[32,384]{1,0:T(8,128)S(1)} %fusion.71), channel_id=1, source_target_pairs={{0,63},{1,0},{2,1},{3,2},{4,3},{5,4},{6,5},{7,6},{8,7},{9,8},{10,9... | collective-permute-start | bytes 147464 | tf_op jit(solution)/shard_map/ppermute | solution.py:13
  571.5 14.7 %collective-permute-start.65 = (f32[32,384]{1,0:T(8,128)S(1)}, f32[32,384]{1,0:T(8,128)S(1)}, u32[]{:S(2)}, u32[]{:S(2)}) collective-permute-start(f32[32,384]{1,0:T(8,128)S(1)} %convolution_multiply_fusion), channel_id=1, source_target_pairs={{0,4},{1,5},{2,6},{3,7},{4,8},{5,9},{6,10},{7,11},{8,12},{9,13},{1... | collective-permute-start | bytes 147464 | tf_op jit(solution)/shard_map/ppermute | solution.py:13
  573.4 16.7 %collective-permute-start.66 = (f32[32,384]{1,0:T(8,128)S(1)}, f32[32,384]{1,0:T(8,128)S(1)}, u32[]{:S(2)}, u32[]{:S(2)}) collective-permute-start(f32[32,384]{1,0:T(8,128)S(1)} %convolution_multiply_fusion), channel_id=1, source_target_pairs={{0,3},{1,4},{2,5},{3,6},{4,7},{5,8},{6,9},{7,10},{8,11},{9,12},{10... | collective-permute-start | bytes 147464 | tf_op jit(solution)/shard_map/ppermute | solution.py:13
  575.3 17.7 %collective-permute-start.67 = (f32[32,384]{1,0:T(8,128)S(1)}, f32[32,384]{1,0:T(8,128)S(1)}, u32[]{:S(2)}, u32[]{:S(2)}) collective-permute-start(f32[32,384]{1,0:T(8,128)S(1)} %convolution_multiply_fusion), channel_id=1, source_target_pairs={{0,2},{1,3},{2,4},{3,5},{4,6},{5,7},{6,8},{7,9},{8,10},{9,11},{10,... | collective-permute-start | bytes 147464 | tf_op jit(solution)/shard_map/ppermute | solution.py:13
  577.3 21.7 %collective-permute-start.68 = (f32[32,384]{1,0:T(8,128)S(1)}, f32[32,384]{1,0:T(8,128)S(1)}, u32[]{:S(2)}, u32[]{:S(2)}) collective-permute-start(f32[32,384]{1,0:T(8,128)S(1)} %convolution_multiply_fusion), channel_id=1, source_target_pairs={{0,1},{1,2},{2,3},{3,4},{4,5},{5,6},{6,7},{7,8},{8,9},{9,10},{10,1... | collective-permute-start | bytes 147464 | tf_op jit(solution)/shard_map/ppermute | solution.py:13
  579.2 22.4 %collective-permute-start.69 = (f32[32,384]{1,0:T(8,128)S(1)}, f32[32,384]{1,0:T(8,128)S(1)}, u32[]{:S(2)}, u32[]{:S(2)}) collective-permute-start(f32[32,384]{1,0:T(8,128)S(1)} %convolution_multiply_fusion), channel_id=1, source_target_pairs={{0,63},{1,0},{2,1},{3,2},{4,3},{5,4},{6,5},{7,6},{8,7},{9,8},{10,9... | collective-permute-start | bytes 147464 | tf_op jit(solution)/shard_map/ppermute | solution.py:13
  586.2 15.4 %collective-permute-start.70 = (f32[32,384]{1,0:T(8,128)S(1)}, f32[32,384]{1,0:T(8,128)S(1)}, u32[]{:S(2)}, u32[]{:S(2)}) collective-permute-start(f32[32,384]{1,0:T(8,128)S(1)} %convolution_multiply_fusion), channel_id=1, source_target_pairs={{0,62},{1,63},{2,0},{3,1},{4,2},{5,3},{6,4},{7,5},{8,6},{9,7},{10,... | collective-permute-start | bytes 147464 | tf_op jit(solution)/shard_map/ppermute | solution.py:13
  (27 other events, 505.2 us)
where the time goes:
time: 864 us; the launch traced here: 862 us
  blocking collectives  501 us (58%)
  starting transfers between devices  258 us (30%)
  matrix products  62.8 us (7%)
  waiting for transfers between devices  19.8 us (2%)
    ppermute x72, starting transfers between devices, from_behind(): lax.ppermute(shard, axis, [(i, (i + by) % size) for i in range(size)])  255 us
    psum x1, blocking collectives, local(): lax.psum(jnp.dot(current, current.T, precision=lax.Precision.HIGHEST), 'r...  251 us
    psum x1, blocking collectives, local(): lax.psum(jnp.dot(lower_rows, basis_raw.T, precision=lax.Precision.HIGHEST...  251 us
    dot_general x9, matrix products, apply_local(): jnp.einsum('vrkc,rkdc->vrd', picked, block_tiles, precision=lax.Precision...  60.9 us
    ppermute x72, waiting for transfers between devices, from_behind(): lax.ppermute(shard, axis, [(i, (i + by) % size) for i in range(size)])  19.8 us
  transfers between devices with their start and end apart: 73, of which 8 were waited for; matrix products, arithmetic and copies ran while one was open for 1% of the time, Pallas kernels for 0%

commit v1 on v0

--- a/solution.py
+++ b/solution.py
@@ -58,7 +58,9 @@
             - previous
         )
         previous, current = (current, following)
-    gram_matrix = lax.psum(jnp.dot(current, current.T, precision=lax.Precision.HIGHEST), "row")
+    gram_matrix = jnp.sum(
+        lax.all_gather(jnp.dot(current, current.T, precision=lax.Precision.HIGHEST), "row"), axis=0
+    )
     factor = jnp.linalg.cholesky(gram_matrix)
     basis_raw = math.sqrt(order_total) * lower_solve(factor, current)
     imaged = apply_local(basis_raw, block_tiles, tile_pattern)

time: 864 us -> 665 us (0.77)
  the two profiles are of different devices: /device:TPU:32 before, /device:TPU:56 now
where the time goes in v1:
time: 665 us; the launch traced here: 663 us
  blocking collectives  302 us (45%)
  starting transfers between devices  257 us (39%)
  matrix products  62.8 us (9%)
  waiting for transfers between devices  21.1 us (3%)
  other arithmetic  8.22 us (1%)
  local copies, waits for them, and re-layouts  7.77 us (1%)
    ppermute x72, starting transfers between devices, from_behind(): lax.ppermute(shard, axis, [(i, (i + by) % size) for i in range(size)])  255 us
    psum x1, blocking collectives, local(): lax.psum(jnp.dot(lower_rows, basis_raw.T, precision=lax.Precision.HIGHEST...  251 us
    dot_general x9, matrix products, apply_local(): jnp.einsum('vrkc,rkdc->vrd', picked, block_tiles, precision=lax.Precision...  60.9 us
    all_gather x1, blocking collectives, local(): lax.all_gather(jnp.dot(current, current.T, precision=lax.Precision.HIGHES...  51.7 us
    ppermute x72, waiting for transfers between devices, from_behind(): lax.ppermute(shard, axis, [(i, (i + by) % size) for i in range(size)])  21.1 us
  transfers between devices with their start and end apart: 73, of which 9 were waited for; matrix products, arithmetic and copies ran while one was open for 1% of the time, Pallas kernels for 0%

profile of v1, /device:TPU:56, one launch (start us, length us, event | category | flops | bytes accessed | tf_op | source)
XLA Modules:
  0.0 662.6 jit_solution(6954247201528074622)
XLA Ops:
  0.6 6.1 collective-permute-start
  6.7 3.4 collective-permute-start.1
  10.2 5.5 collective-permute-start.2
  15.7 3.5 collective-permute-start.3
  19.2 5.4 collective-permute-start.4
  31.8 5.5 collective-permute-start.7
  40.6 6.7 %fusion.16 = f32[3,32,128,1]{2,1,3,0:T(8,128)S(1)} fusion(f32[3,24,128,128]{3,2,1,0:T(8,128)} %param.8, f32[3,24,32,128]{3,2,1,0:T(8,128)S(1)} %bitcast.378, pred[3,24]{1,0:T(4,128)(4,1)S(1)} %get-tuple-element.5), kind=kOutput, calls=%fused_computation.25 | convolution fusion | flops 453279744 | bytes 5947464 | tf_op jit(solution)/shard_map/vrkc,rkdc->vrd/dot_general | solution.py:40
  47.3 4.9 collective-permute-start.8
  58.4 6.5 collective-permute-start.12
  65.0 3.9 collective-permute-start.13
  71.7 3.7 collective-permute-start.15
  75.6 3.8 collective-permute-done.15
  80.1 6.7 %fusion.14 = f32[3,32,128,1]{2,1,3,0:T(8,128)S(1)} fusion(f32[3,24,128,128]{3,2,1,0:T(8,128)} %param.8, f32[3,24,32,128]{3,2,1,0:T(8,128)S(1)} %bitcast.379, pred[3,24]{1,0:T(4,128)(4,1)S(1)} %get-tuple-element.5), kind=kOutput, calls=%fused_computation.23 | convolution fusion | flops 453279744 | bytes 5947464 | tf_op jit(solution)/shard_map/vrkc,rkdc->vrd/dot_general | solution.py:40
  96.0 6.7 %collective-permute-start.20 = (f32[32,384]{1,0:T(8,128)S(1)}, f32[32,384]{1,0:T(8,128)S(1)}, u32[]{:S(2)}, u32[]{:S(2)}) collective-permute-start(f32[32,384]{1,0:T(8,128)S(1)} %fusion.86), channel_id=1, source_target_pairs={{0,63},{1,0},{2,1},{3,2},{4,3},{5,4},{6,5},{7,6},{8,7},{9,8},{10,9... | collective-permute-start | bytes 147464 | tf_op jit(solution)/shard_map/ppermute | solution.py:13
  102.8 3.5 collective-permute-start.21
  106.3 2.8 collective-permute-start.22
  109.2 5.1 collective-permute-start.23
  114.4 3.0 collective-permute-done.23
  118.2 6.7 %fusion.12 = f32[3,32,128,1]{2,1,3,0:T(8,128)S(1)} fusion(f32[3,24,128,128]{3,2,1,0:T(8,128)} %param.8, f32[3,24,32,128]{3,2,1,0:T(8,128)S(1)} %bitcast.380, pred[3,24]{1,0:T(4,128)(4,1)S(1)} %get-tuple-element.5), kind=kOutput, calls=%fused_computation.21 | convolution fusion | flops 453279744 | bytes 5947464 | tf_op jit(solution)/shard_map/vrkc,rkdc->vrd/dot_general | solution.py:40
  133.3 6.8 %collective-permute-start.28 = (f32[32,384]{1,0:T(8,128)S(1)}, f32[32,384]{1,0:T(8,128)S(1)}, u32[]{:S(2)}, u32[]{:S(2)}) collective-permute-start(f32[32,384]{1,0:T(8,128)S(1)} %fusion.83), channel_id=1, source_target_pairs={{0,63},{1,0},{2,1},{3,2},{4,3},{5,4},{6,5},{7,6},{8,7},{9,8},{10,9... | collective-permute-start | bytes 147464 | tf_op jit(solution)/shard_map/ppermute | solution.py:13
  140.0 3.9 collective-permute-start.29
  146.8 5.6 collective-permute-start.31
  155.4 6.7 %fusion.10 = f32[3,32,128,1]{2,1,3,0:T(8,128)S(1)} fusion(f32[3,24,128,128]{3,2,1,0:T(8,128)} %param.8, f32[3,24,32,128]{3,2,1,0:T(8,128)S(1)} %bitcast.381, pred[3,24]{1,0:T(4,128)(4,1)S(1)} %get-tuple-element.5), kind=kOutput, calls=%fused_computation.19 | convolution fusion | flops 453279744 | bytes 5947464 | tf_op jit(solution)/shard_map/vrkc,rkdc->vrd/dot_general | solution.py:40
  171.2 6.6 collective-permute-start.36
  177.8 3.6 collective-permute-start.37
  181.4 2.8 collective-permute-start.38
  184.3 6.1 collective-permute-start.39
  193.2 6.7 %fusion.8 = f32[3,32,128,1]{2,1,3,0:T(8,128)S(1)} fusion(f32[3,24,128,128]{3,2,1,0:T(8,128)} %param.8, f32[3,24,32,128]{3,2,1,0:T(8,128)S(1)} %bitcast.382, pred[3,24]{1,0:T(4,128)(4,1)S(1)} %get-tuple-element.5), kind=kOutput, calls=%fused_computation.17 | convolution fusion | flops 453279744 | bytes 5947464 | tf_op jit(solution)/shard_map/vrkc,rkdc->vrd/dot_general | solution.py:40
  208.7 6.6 collective-permute-start.44
  215.3 3.7 collective-permute-start.45
  221.9 6.0 collective-permute-start.47
  230.7 6.7 %fusion.6 = f32[3,32,128,1]{2,1,3,0:T(8,128)S(1)} fusion(f32[3,24,128,128]{3,2,1,0:T(8,128)} %param.8, f32[3,24,32,128]{3,2,1,0:T(8,128)S(1)} %bitcast.383, pred[3,24]{1,0:T(4,128)(4,1)S(1)} %get-tuple-element.5), kind=kOutput, calls=%fused_computation.15 | convolution fusion | flops 453279744 | bytes 5947464 | tf_op jit(solution)/shard_map/vrkc,rkdc->vrd/dot_general | solution.py:40
  246.5 6.6 collective-permute-start.52
  253.1 3.5 collective-permute-start.53
  256.6 2.8 collective-permute-start.54
  259.5 6.0 collective-permute-start.55
  268.5 6.7 %fusion.4 = f32[3,32,128,1]{2,1,3,0:T(8,128)S(1)} fusion(f32[3,24,128,128]{3,2,1,0:T(8,128)} %param.8, f32[3,24,32,128]{3,2,1,0:T(8,128)S(1)} %bitcast.384, pred[3,24]{1,0:T(4,128)(4,1)S(1)} %get-tuple-element.5), kind=kOutput, calls=%fused_computation.13 | convolution fusion | flops 453279744 | bytes 5947464 | tf_op jit(solution)/shard_map/vrkc,rkdc->vrd/dot_general | solution.py:40
  284.1 6.6 collective-permute-start.60
  290.7 3.7 collective-permute-start.61
  297.1 6.0 collective-permute-start.63
  306.1 7.2 %fusion.43 = f32[32,3,128]{2,0,1:T(8,128)S(1)} fusion(f32[3,24,128,128]{3,2,1,0:T(8,128)} %param.8, f32[3,24,32,128]{3,2,1,0:T(8,128)S(1)} %bitcast.376, pred[3,24]{1,0:T(4,128)(4,1)S(1)} %get-tuple-element.5, f32[3,32,128,1]{2,1,3,0:T(8,128)S(1)} %fusion.4, f32[3,32,128,1]{2,1,3,0:T(8,128)S(1)} %fusion.6, f32[3,32,128,1]{2,1,3,0:T(8,128)S(1)} %fusion.8, ...), kind=kOutput, calls=%fused_computation.44 | convolution fusion | flops 453746688 | bytes 6340688 | tf_op jit(solution)/shard_map/vrkc,rkdc->vrd/dot_general | solution.py:40
  313.5 51.7 %all-gather = f32[2048,32]{1,0:T(8,128)S(1)} all-gather(f32[32,32]{1,0:T(8,128)S(1)} %convolution_bitcast_fusion), channel_id=2, replica_groups=mesh['cuts'=8,'row'=64] {'row'}, dimensions={0}, use_global_device_ids=true | all-gather | bytes 266240 | tf_op jit(solution)/shard_map/all_gather | solution.py:62
  365.4 2.9 cholesky.16
  376.6 4.7 collective-permute-start.67
  383.2 7.0 %collective-permute-start.69 = (f32[32,384]{1,0:T(8,128)S(1)}, f32[32,384]{1,0:T(8,128)S(1)}, u32[]{:S(2)}, u32[]{:S(2)}) collective-permute-start(f32[32,384]{1,0:T(8,128)S(1)} %convolution_multiply_fusion), channel_id=1, source_target_pairs={{0,63},{1,0},{2,1},{3,2},{4,3},{5,4},{6,5},{7,6},{8,7},{9,8},{10,9... | collective-permute-start | bytes 147464 | tf_op jit(solution)/shard_map/ppermute | solution.py:13
  394.1 5.7 collective-permute-start.72
  403.3 6.7 %fusion.30 = f32[3,4,8,128]{3,2,1,0:T(8,128)S(1)} fusion(f32[3,24,128,128]{3,2,1,0:T(8,128)} %param.8, f32[3,24,32,128]{3,2,1,0:T(8,128)S(1)} %bitcast.377, pred[3,24]{1,0:T(4,128)(4,1)S(1)} %get-tuple-element.5), kind=kOutput, calls=%fused_computation.37 | convolution fusion | flops 453279744 | bytes 5947464 | tf_op jit(solution)/shard_map/vrkc,rkdc->vrd/dot_general | solution.py:40
  410.5 250.5 %all-reduce = (f32[8,32]{1,0:T(8,128)S(1)}, f32[32,32]{1,0:T(8,128)S(1)}) all-reduce(f32[8,32]{1,0:T(8,128)S(1)} %fusion.129, f32[32,32]{1,0:T(8,128)S(1)} %fusion.64), channel_id=1, replica_groups=mesh['cuts'=8,'row'=64] {'row'}, use_global_device_ids=true, to_apply=%region_3.5 | all-reduce | flops 1280 | bytes 10240 | tf_op jit(solution)/shard_map/psum | solution.py:79
  (238 shorter events, 115.0 us)
Async XLA Ops:
  0.6 26.9 %collective-permute-start = (f32[32,384]{1,0:T(8,128)}, f32[32,384]{1,0:T(8,128)S(1)}, u32[]{:S(2)}, u32[]{:S(2)}) collective-permute-start(f32[32,384]{1,0:T(8,128)} %bitcast.386), channel_id=1, source_target_pairs={{0,4},{1,5},{2,6},{3,7},{4,8},{5,9},{6,10},{7,11},{8,12},{9,13},{1... | collective-permute-start | bytes 147464 | tf_op jit(solution)/shard_map/ppermute | solution.py:13
  6.7 23.1 %collective-permute-start.1 = (f32[32,384]{1,0:T(8,128)}, f32[32,384]{1,0:T(8,128)S(1)}, u32[]{:S(2)}, u32[]{:S(2)}) collective-permute-start(f32[32,384]{1,0:T(8,128)} %bitcast.387), channel_id=1, source_target_pairs={{0,3},{1,4},{2,5},{3,6},{4,7},{5,8},{6,9},{7,10},{8,11},{9,12},{10... | collective-permute-start | bytes 147464 | tf_op jit(solution)/shard_map/ppermute | solution.py:13
  10.2 21.6 %collective-permute-start.2 = (f32[32,384]{1,0:T(8,128)}, f32[32,384]{1,0:T(8,128)S(1)}, u32[]{:S(2)}, u32[]{:S(2)}) collective-permute-start(f32[32,384]{1,0:T(8,128)} %bitcast.388), channel_id=1, source_target_pairs={{0,2},{1,3},{2,4},{3,5},{4,6},{5,7},{6,8},{7,9},{8,10},{9,11},{10,... | collective-permute-start | bytes 147464 | tf_op jit(solution)/shard_map/ppermute | solution.py:13
  15.7 21.6 %collective-permute-start.3 = (f32[32,384]{1,0:T(8,128)}, f32[32,384]{1,0:T(8,128)S(1)}, u32[]{:S(2)}, u32[]{:S(2)}) collective-permute-start(f32[32,384]{1,0:T(8,128)} %bitcast.389), channel_id=1, source_target_pairs={{0,1},{1,2},{2,3},{3,4},{4,5},{5,6},{6,7},{7,8},{8,9},{9,10},{10,1... | collective-permute-start | bytes 147464 | tf_op jit(solution)/shard_map/ppermute | solution.py:13
  19.2 18.1 %collective-permute-start.4 = (f32[32,384]{1,0:T(8,128)}, f32[32,384]{1,0:T(8,128)S(1)}, u32[]{:S(2)}, u32[]{:S(2)}) collective-permute-start(f32[32,384]{1,0:T(8,128)} %bitcast.390), channel_id=1, source_target_pairs={{0,63},{1,0},{2,1},{3,2},{4,3},{5,4},{6,5},{7,6},{8,7},{9,8},{10,9... | collective-permute-start | bytes 147464 | tf_op jit(solution)/shard_map/ppermute | solution.py:13
  47.3 17.7 %collective-permute-start.8 = (f32[32,384]{1,0:T(8,128)S(1)}, f32[32,384]{1,0:T(8,128)S(1)}, u32[]{:S(2)}, u32[]{:S(2)}) collective-permute-start(f32[32,384]{1,0:T(8,128)S(1)} %fusion.87), channel_id=1, source_target_pairs={{0,4},{1,5},{2,6},{3,7},{4,8},{5,9},{6,10},{7,11},{8,12},{9,13},{1... | collective-permute-start | bytes 147464 | tf_op jit(solution)/shard_map/ppermute | solution.py:13
  52.2 16.7 %collective-permute-start.9 = (f32[32,384]{1,0:T(8,128)S(1)}, f32[32,384]{1,0:T(8,128)S(1)}, u32[]{:S(2)}, u32[]{:S(2)}) collective-permute-start(f32[32,384]{1,0:T(8,128)S(1)} %fusion.87), channel_id=1, source_target_pairs={{0,3},{1,4},{2,5},{3,6},{4,7},{5,8},{6,9},{7,10},{8,11},{9,12},{10... | collective-permute-start | bytes 147464 | tf_op jit(solution)/shard_map/ppermute | solution.py:13
  54.1 17.6 %collective-permute-start.10 = (f32[32,384]{1,0:T(8,128)S(1)}, f32[32,384]{1,0:T(8,128)S(1)}, u32[]{:S(2)}, u32[]{:S(2)}) collective-permute-start(f32[32,384]{1,0:T(8,128)S(1)} %fusion.87), channel_id=1, source_target_pairs={{0,2},{1,3},{2,4},{3,5},{4,6},{5,7},{6,8},{7,9},{8,10},{9,11},{10,... | collective-permute-start | bytes 147464 | tf_op jit(solution)/shard_map/ppermute | solution.py:13
  56.1 19.4 %collective-permute-start.11 = (f32[32,384]{1,0:T(8,128)S(1)}, f32[32,384]{1,0:T(8,128)S(1)}, u32[]{:S(2)}, u32[]{:S(2)}) collective-permute-start(f32[32,384]{1,0:T(8,128)S(1)} %fusion.87), channel_id=1, source_target_pairs={{0,1},{1,2},{2,3},{3,4},{4,5},{5,6},{6,7},{7,8},{8,9},{9,10},{10,1... | collective-permute-start | bytes 147464 | tf_op jit(solution)/shard_map/ppermute | solution.py:13
  58.4 17.1 %collective-permute-start.12 = (f32[32,384]{1,0:T(8,128)S(1)}, f32[32,384]{1,0:T(8,128)S(1)}, u32[]{:S(2)}, u32[]{:S(2)}) collective-permute-start(f32[32,384]{1,0:T(8,128)S(1)} %fusion.87), channel_id=1, source_target_pairs={{0,63},{1,0},{2,1},{3,2},{4,3},{5,4},{6,5},{7,6},{8,7},{9,8},{10,9... | collective-permute-start | bytes 147464 | tf_op jit(solution)/shard_map/ppermute | solution.py:13
  86.8 15.9 %collective-permute-start.16 = (f32[32,384]{1,0:T(8,128)S(1)}, f32[32,384]{1,0:T(8,128)S(1)}, u32[]{:S(2)}, u32[]{:S(2)}) collective-permute-start(f32[32,384]{1,0:T(8,128)S(1)} %fusion.86), channel_id=1, source_target_pairs={{0,4},{1,5},{2,6},{3,7},{4,8},{5,9},{6,10},{7,11},{8,12},{9,13},{1... | collective-permute-start | bytes 147464 | tf_op jit(solution)/shard_map/ppermute | solution.py:13
  89.6 16.7 %collective-permute-start.17 = (f32[32,384]{1,0:T(8,128)S(1)}, f32[32,384]{1,0:T(8,128)S(1)}, u32[]{:S(2)}, u32[]{:S(2)}) collective-permute-start(f32[32,384]{1,0:T(8,128)S(1)} %fusion.86), channel_id=1, source_target_pairs={{0,3},{1,4},{2,5},{3,6},{4,7},{5,8},{6,9},{7,10},{8,11},{9,12},{10... | collective-permute-start | bytes 147464 | tf_op jit(solution)/shard_map/ppermute | solution.py:13
  91.5 17.6 %collective-permute-start.18 = (f32[32,384]{1,0:T(8,128)S(1)}, f32[32,384]{1,0:T(8,128)S(1)}, u32[]{:S(2)}, u32[]{:S(2)}) collective-permute-start(f32[32,384]{1,0:T(8,128)S(1)} %fusion.86), channel_id=1, source_target_pairs={{0,2},{1,3},{2,4},{3,5},{4,6},{5,7},{6,8},{7,9},{8,10},{9,11},{10,... | collective-permute-start | bytes 147464 | tf_op jit(solution)/shard_map/ppermute | solution.py:13
  93.9 20.5 %collective-permute-start.19 = (f32[32,384]{1,0:T(8,128)S(1)}, f32[32,384]{1,0:T(8,128)S(1)}, u32[]{:S(2)}, u32[]{:S(2)}) collective-permute-start(f32[32,384]{1,0:T(8,128)S(1)} %fusion.86), channel_id=1, source_target_pairs={{0,1},{1,2},{2,3},{3,4},{4,5},{5,6},{6,7},{7,8},{8,9},{9,10},{10,1... | collective-permute-start | bytes 147464 | tf_op jit(solution)/shard_map/ppermute | solution.py:13
  96.0 18.3 %collective-permute-start.20 = (f32[32,384]{1,0:T(8,128)S(1)}, f32[32,384]{1,0:T(8,128)S(1)}, u32[]{:S(2)}, u32[]{:S(2)}) collective-permute-start(f32[32,384]{1,0:T(8,128)S(1)} %fusion.86), channel_id=1, source_target_pairs={{0,63},{1,0},{2,1},{3,2},{4,3},{5,4},{6,5},{7,6},{8,7},{9,8},{10,9... | collective-permute-start | bytes 147464 | tf_op jit(solution)/shard_map/ppermute | solution.py:13
  124.9 15.1 %collective-permute-start.24 = (f32[32,384]{1,0:T(8,128)S(1)}, f32[32,384]{1,0:T(8,128)S(1)}, u32[]{:S(2)}, u32[]{:S(2)}) collective-permute-start(f32[32,384]{1,0:T(8,128)S(1)} %fusion.83), channel_id=1, source_target_pairs={{0,4},{1,5},{2,6},{3,7},{4,8},{5,9},{6,10},{7,11},{8,12},{9,13},{1... | collective-permute-start | bytes 147464 | tf_op jit(solution)/shard_map/ppermute | solution.py:13
  127.3 16.7 %collective-permute-start.25 = (f32[32,384]{1,0:T(8,128)S(1)}, f32[32,384]{1,0:T(8,128)S(1)}, u32[]{:S(2)}, u32[]{:S(2)}) collective-permute-start(f32[32,384]{1,0:T(8,128)S(1)} %fusion.83), channel_id=1, source_target_pairs={{0,3},{1,4},{2,5},{3,6},{4,7},{5,8},{6,9},{7,10},{8,11},{9,12},{10... | collective-permute-start | bytes 147464 | tf_op jit(solution)/shard_map/ppermute | solution.py:13
  129.2 17.6 %collective-permute-start.26 = (f32[32,384]{1,0:T(8,128)S(1)}, f32[32,384]{1,0:T(8,128)S(1)}, u32[]{:S(2)}, u32[]{:S(2)}) collective-permute-start(f32[32,384]{1,0:T(8,128)S(1)} %fusion.83), channel_id=1, source_target_pairs={{0,2},{1,3},{2,4},{3,5},{4,6},{5,7},{6,8},{7,9},{8,10},{9,11},{10,... | collective-permute-start | bytes 147464 | tf_op jit(solution)/shard_map/ppermute | solution.py:13
  131.1 21.2 %collective-permute-start.27 = (f32[32,384]{1,0:T(8,128)S(1)}, f32[32,384]{1,0:T(8,128)S(1)}, u32[]{:S(2)}, u32[]{:S(2)}) collective-permute-start(f32[32,384]{1,0:T(8,128)S(1)} %fusion.83), channel_id=1, source_target_pairs={{0,1},{1,2},{2,3},{3,4},{4,5},{5,6},{6,7},{7,8},{8,9},{9,10},{10,1... | collective-permute-start | bytes 147464 | tf_op jit(solution)/shard_map/ppermute | solution.py:13
  133.3 19.2 %collective-permute-start.28 = (f32[32,384]{1,0:T(8,128)S(1)}, f32[32,384]{1,0:T(8,128)S(1)}, u32[]{:S(2)}, u32[]{:S(2)}) collective-permute-start(f32[32,384]{1,0:T(8,128)S(1)} %fusion.83), channel_id=1, source_target_pairs={{0,63},{1,0},{2,1},{3,2},{4,3},{5,4},{6,5},{7,6},{8,7},{9,8},{10,9... | collective-permute-start | bytes 147464 | tf_op jit(solution)/shard_map/ppermute | solution.py:13
  162.1 15.7 %collective-permute-start.32 = (f32[32,384]{1,0:T(8,128)S(1)}, f32[32,384]{1,0:T(8,128)S(1)}, u32[]{:S(2)}, u32[]{:S(2)}) collective-permute-start(f32[32,384]{1,0:T(8,128)S(1)} %fusion.80), channel_id=1, source_target_pairs={{0,4},{1,5},{2,6},{3,7},{4,8},{5,9},{6,10},{7,11},{8,12},{9,13},{1... | collective-permute-start | bytes 147464 | tf_op jit(solution)/shard_map/ppermute | solution.py:13
  164.7 16.7 %collective-permute-start.33 = (f32[32,384]{1,0:T(8,128)S(1)}, f32[32,384]{1,0:T(8,128)S(1)}, u32[]{:S(2)}, u32[]{:S(2)}) collective-permute-start(f32[32,384]{1,0:T(8,128)S(1)} %fusion.80), channel_id=1, source_target_pairs={{0,3},{1,4},{2,5},{3,6},{4,7},{5,8},{6,9},{7,10},{8,11},{9,12},{10... | collective-permute-start | bytes 147464 | tf_op jit(solution)/shard_map/ppermute | solution.py:13
  166.6 17.6 %collective-permute-start.34 = (f32[32,384]{1,0:T(8,128)S(1)}, f32[32,384]{1,0:T(8,128)S(1)}, u32[]{:S(2)}, u32[]{:S(2)}) collective-permute-start(f32[32,384]{1,0:T(8,128)S(1)} %fusion.80), channel_id=1, source_target_pairs={{0,2},{1,3},{2,4},{3,5},{4,6},{5,7},{6,8},{7,9},{8,10},{9,11},{10,... | collective-permute-start | bytes 147464 | tf_op jit(solution)/shard_map/ppermute | solution.py:13
  168.8 21.6 %collective-permute-start.35 = (f32[32,384]{1,0:T(8,128)S(1)}, f32[32,384]{1,0:T(8,128)S(1)}, u32[]{:S(2)}, u32[]{:S(2)}) collective-permute-start(f32[32,384]{1,0:T(8,128)S(1)} %fusion.80), channel_id=1, source_target_pairs={{0,1},{1,2},{2,3},{3,4},{4,5},{5,6},{6,7},{7,8},{8,9},{9,10},{10,1... | collective-permute-start | bytes 147464 | tf_op jit(solution)/shard_map/ppermute | solution.py:13
  171.2 19.2 %collective-permute-start.36 = (f32[32,384]{1,0:T(8,128)S(1)}, f32[32,384]{1,0:T(8,128)S(1)}, u32[]{:S(2)}, u32[]{:S(2)}) collective-permute-start(f32[32,384]{1,0:T(8,128)S(1)} %fusion.80), channel_id=1, source_target_pairs={{0,63},{1,0},{2,1},{3,2},{4,3},{5,4},{6,5},{7,6},{8,7},{9,8},{10,9... | collective-permute-start | bytes 147464 | tf_op jit(solution)/shard_map/ppermute | solution.py:13
  177.8 12.7 %collective-permute-start.37 = (f32[32,384]{1,0:T(8,128)S(1)}, f32[32,384]{1,0:T(8,128)S(1)}, u32[]{:S(2)}, u32[]{:S(2)}) collective-permute-start(f32[32,384]{1,0:T(8,128)S(1)} %fusion.80), channel_id=1, source_target_pairs={{0,62},{1,63},{2,0},{3,1},{4,2},{5,3},{6,4},{7,5},{8,6},{9,7},{10,... | collective-permute-start | bytes 147464 | tf_op jit(solution)/shard_map/ppermute | solution.py:13
  200.0 15.3 %collective-permute-start.40 = (f32[32,384]{1,0:T(8,128)S(1)}, f32[32,384]{1,0:T(8,128)S(1)}, u32[]{:S(2)}, u32[]{:S(2)}) collective-permute-start(f32[32,384]{1,0:T(8,128)S(1)} %fusion.77), channel_id=1, source_target_pairs={{0,4},{1,5},{2,6},{3,7},{4,8},{5,9},{6,10},{7,11},{8,12},{9,13},{1... | collective-permute-start | bytes 147464 | tf_op jit(solution)/shard_map/ppermute | solution.py:13
  202.3 16.7 %collective-permute-start.41 = (f32[32,384]{1,0:T(8,128)S(1)}, f32[32,384]{1,0:T(8,128)S(1)}, u32[]{:S(2)}, u32[]{:S(2)}) collective-permute-start(f32[32,384]{1,0:T(8,128)S(1)} %fusion.77), channel_id=1, source_target_pairs={{0,3},{1,4},{2,5},{3,6},{4,7},{5,8},{6,9},{7,10},{8,11},{9,12},{10... | collective-permute-start | bytes 147464 | tf_op jit(solution)/shard_map/ppermute | solution.py:13
  204.3 17.6 %collective-permute-start.42 = (f32[32,384]{1,0:T(8,128)S(1)}, f32[32,384]{1,0:T(8,128)S(1)}, u32[]{:S(2)}, u32[]{:S(2)}) collective-permute-start(f32[32,384]{1,0:T(8,128)S(1)} %fusion.77), channel_id=1, source_target_pairs={{0,2},{1,3},{2,4},{3,5},{4,6},{5,7},{6,8},{7,9},{8,10},{9,11},{10,... | collective-permute-start | bytes 147464 | tf_op jit(solution)/shard_map/ppermute | solution.py:13
  206.2 21.7 %collective-permute-start.43 = (f32[32,384]{1,0:T(8,128)S(1)}, f32[32,384]{1,0:T(8,128)S(1)}, u32[]{:S(2)}, u32[]{:S(2)}) collective-permute-start(f32[32,384]{1,0:T(8,128)S(1)} %fusion.77), channel_id=1, source_target_pairs={{0,1},{1,2},{2,3},{3,4},{4,5},{5,6},{6,7},{7,8},{8,9},{9,10},{10,1... | collective-permute-start | bytes 147464 | tf_op jit(solution)/shard_map/ppermute | solution.py:13
  208.7 19.2 %collective-permute-start.44 = (f32[32,384]{1,0:T(8,128)S(1)}, f32[32,384]{1,0:T(8,128)S(1)}, u32[]{:S(2)}, u32[]{:S(2)}) collective-permute-start(f32[32,384]{1,0:T(8,128)S(1)} %fusion.77), channel_id=1, source_target_pairs={{0,63},{1,0},{2,1},{3,2},{4,3},{5,4},{6,5},{7,6},{8,7},{9,8},{10,9... | collective-permute-start | bytes 147464 | tf_op jit(solution)/shard_map/ppermute | solution.py:13
  215.3 12.7 %collective-permute-start.45 = (f32[32,384]{1,0:T(8,128)S(1)}, f32[32,384]{1,0:T(8,128)S(1)}, u32[]{:S(2)}, u32[]{:S(2)}) collective-permute-start(f32[32,384]{1,0:T(8,128)S(1)} %fusion.77), channel_id=1, source_target_pairs={{0,62},{1,63},{2,0},{3,1},{4,2},{5,3},{6,4},{7,5},{8,6},{9,7},{10,... | collective-permute-start | bytes 147464 | tf_op jit(solution)/shard_map/ppermute | solution.py:13
  237.4 15.7 %collective-permute-start.48 = (f32[32,384]{1,0:T(8,128)S(1)}, f32[32,384]{1,0:T(8,128)S(1)}, u32[]{:S(2)}, u32[]{:S(2)}) collective-permute-start(f32[32,384]{1,0:T(8,128)S(1)} %fusion.74), channel_id=1, source_target_pairs={{0,4},{1,5},{2,6},{3,7},{4,8},{5,9},{6,10},{7,11},{8,12},{9,13},{1... | collective-permute-start | bytes 147464 | tf_op jit(solution)/shard_map/ppermute | solution.py:13
  239.9 16.7 %collective-permute-start.49 = (f32[32,384]{1,0:T(8,128)S(1)}, f32[32,384]{1,0:T(8,128)S(1)}, u32[]{:S(2)}, u32[]{:S(2)}) collective-permute-start(f32[32,384]{1,0:T(8,128)S(1)} %fusion.74), channel_id=1, source_target_pairs={{0,3},{1,4},{2,5},{3,6},{4,7},{5,8},{6,9},{7,10},{8,11},{9,12},{10... | collective-permute-start | bytes 147464 | tf_op jit(solution)/shard_map/ppermute | solution.py:13
  241.9 17.6 %collective-permute-start.50 = (f32[32,384]{1,0:T(8,128)S(1)}, f32[32,384]{1,0:T(8,128)S(1)}, u32[]{:S(2)}, u32[]{:S(2)}) collective-permute-start(f32[32,384]{1,0:T(8,128)S(1)} %fusion.74), channel_id=1, source_target_pairs={{0,2},{1,3},{2,4},{3,5},{4,6},{5,7},{6,8},{7,9},{8,10},{9,11},{10,... | collective-permute-start | bytes 147464 | tf_op jit(solution)/shard_map/ppermute | solution.py:13
  244.2 21.3 %collective-permute-start.51 = (f32[32,384]{1,0:T(8,128)S(1)}, f32[32,384]{1,0:T(8,128)S(1)}, u32[]{:S(2)}, u32[]{:S(2)}) collective-permute-start(f32[32,384]{1,0:T(8,128)S(1)} %fusion.74), channel_id=1, source_target_pairs={{0,1},{1,2},{2,3},{3,4},{4,5},{5,6},{6,7},{7,8},{8,9},{9,10},{10,1... | collective-permute-start | bytes 147464 | tf_op jit(solution)/shard_map/ppermute | solution.py:13
  246.5 19.1 %collective-permute-start.52 = (f32[32,384]{1,0:T(8,128)S(1)}, f32[32,384]{1,0:T(8,128)S(1)}, u32[]{:S(2)}, u32[]{:S(2)}) collective-permute-start(f32[32,384]{1,0:T(8,128)S(1)} %fusion.74), channel_id=1, source_target_pairs={{0,63},{1,0},{2,1},{3,2},{4,3},{5,4},{6,5},{7,6},{8,7},{9,8},{10,9... | collective-permute-start | bytes 147464 | tf_op jit(solution)/shard_map/ppermute | solution.py:13
  275.2 15.4 %collective-permute-start.56 = (f32[32,384]{1,0:T(8,128)S(1)}, f32[32,384]{1,0:T(8,128)S(1)}, u32[]{:S(2)}, u32[]{:S(2)}) collective-permute-start(f32[32,384]{1,0:T(8,128)S(1)} %fusion.71), channel_id=1, source_target_pairs={{0,4},{1,5},{2,6},{3,7},{4,8},{5,9},{6,10},{7,11},{8,12},{9,13},{1... | collective-permute-start | bytes 147464 | tf_op jit(solution)/shard_map/ppermute | solution.py:13
  277.6 16.7 %collective-permute-start.57 = (f32[32,384]{1,0:T(8,128)S(1)}, f32[32,384]{1,0:T(8,128)S(1)}, u32[]{:S(2)}, u32[]{:S(2)}) collective-permute-start(f32[32,384]{1,0:T(8,128)S(1)} %fusion.71), channel_id=1, source_target_pairs={{0,3},{1,4},{2,5},{3,6},{4,7},{5,8},{6,9},{7,10},{8,11},{9,12},{10... | collective-permute-start | bytes 147464 | tf_op jit(solution)/shard_map/ppermute | solution.py:13
  279.6 17.6 %collective-permute-start.58 = (f32[32,384]{1,0:T(8,128)S(1)}, f32[32,384]{1,0:T(8,128)S(1)}, u32[]{:S(2)}, u32[]{:S(2)}) collective-permute-start(f32[32,384]{1,0:T(8,128)S(1)} %fusion.71), channel_id=1, source_target_pairs={{0,2},{1,3},{2,4},{3,5},{4,6},{5,7},{6,8},{7,9},{8,10},{9,11},{10,... | collective-permute-start | bytes 147464 | tf_op jit(solution)/shard_map/ppermute | solution.py:13
  281.6 21.5 %collective-permute-start.59 = (f32[32,384]{1,0:T(8,128)S(1)}, f32[32,384]{1,0:T(8,128)S(1)}, u32[]{:S(2)}, u32[]{:S(2)}) collective-permute-start(f32[32,384]{1,0:T(8,128)S(1)} %fusion.71), channel_id=1, source_target_pairs={{0,1},{1,2},{2,3},{3,4},{4,5},{5,6},{6,7},{7,8},{8,9},{9,10},{10,1... | collective-permute-start | bytes 147464 | tf_op jit(solution)/shard_map/ppermute | solution.py:13
  284.1 19.1 %collective-permute-start.60 = (f32[32,384]{1,0:T(8,128)S(1)}, f32[32,384]{1,0:T(8,128)S(1)}, u32[]{:S(2)}, u32[]{:S(2)}) collective-permute-start(f32[32,384]{1,0:T(8,128)S(1)} %fusion.71), channel_id=1, source_target_pairs={{0,63},{1,0},{2,1},{3,2},{4,3},{5,4},{6,5},{7,6},{8,7},{9,8},{10,9... | collective-permute-start | bytes 147464 | tf_op jit(solution)/shard_map/ppermute | solution.py:13
  290.7 12.5 %collective-permute-start.61 = (f32[32,384]{1,0:T(8,128)S(1)}, f32[32,384]{1,0:T(8,128)S(1)}, u32[]{:S(2)}, u32[]{:S(2)}) collective-permute-start(f32[32,384]{1,0:T(8,128)S(1)} %fusion.71), channel_id=1, source_target_pairs={{0,62},{1,63},{2,0},{3,1},{4,2},{5,3},{6,4},{7,5},{8,6},{9,7},{10,... | collective-permute-start | bytes 147464 | tf_op jit(solution)/shard_map/ppermute | solution.py:13
  372.4 17.9 %collective-permute-start.65 = (f32[32,384]{1,0:T(8,128)S(1)}, f32[32,384]{1,0:T(8,128)S(1)}, u32[]{:S(2)}, u32[]{:S(2)}) collective-permute-start(f32[32,384]{1,0:T(8,128)S(1)} %convolution_multiply_fusion), channel_id=1, source_target_pairs={{0,4},{1,5},{2,6},{3,7},{4,8},{5,9},{6,10},{7,11},{8,12},{9,13},{1... | collective-permute-start | bytes 147464 | tf_op jit(solution)/shard_map/ppermute | solution.py:13
  374.6 17.6 %collective-permute-start.66 = (f32[32,384]{1,0:T(8,128)S(1)}, f32[32,384]{1,0:T(8,128)S(1)}, u32[]{:S(2)}, u32[]{:S(2)}) collective-permute-start(f32[32,384]{1,0:T(8,128)S(1)} %convolution_multiply_fusion), channel_id=1, source_target_pairs={{0,3},{1,4},{2,5},{3,6},{4,7},{5,8},{6,9},{7,10},{8,11},{9,12},{10... | collective-permute-start | bytes 147464 | tf_op jit(solution)/shard_map/ppermute | solution.py:13
  376.6 17.5 %collective-permute-start.67 = (f32[32,384]{1,0:T(8,128)S(1)}, f32[32,384]{1,0:T(8,128)S(1)}, u32[]{:S(2)}, u32[]{:S(2)}) collective-permute-start(f32[32,384]{1,0:T(8,128)S(1)} %convolution_multiply_fusion), channel_id=1, source_target_pairs={{0,2},{1,3},{2,4},{3,5},{4,6},{5,7},{6,8},{7,9},{8,10},{9,11},{10,... | collective-permute-start | bytes 147464 | tf_op jit(solution)/shard_map/ppermute | solution.py:13
  381.3 18.6 %collective-permute-start.68 = (f32[32,384]{1,0:T(8,128)S(1)}, f32[32,384]{1,0:T(8,128)S(1)}, u32[]{:S(2)}, u32[]{:S(2)}) collective-permute-start(f32[32,384]{1,0:T(8,128)S(1)} %convolution_multiply_fusion), channel_id=1, source_target_pairs={{0,1},{1,2},{2,3},{3,4},{4,5},{5,6},{6,7},{7,8},{8,9},{9,10},{10,1... | collective-permute-start | bytes 147464 | tf_op jit(solution)/shard_map/ppermute | solution.py:13
  383.2 18.0 %collective-permute-start.69 = (f32[32,384]{1,0:T(8,128)S(1)}, f32[32,384]{1,0:T(8,128)S(1)}, u32[]{:S(2)}, u32[]{:S(2)}) collective-permute-start(f32[32,384]{1,0:T(8,128)S(1)} %convolution_multiply_fusion), channel_id=1, source_target_pairs={{0,63},{1,0},{2,1},{3,2},{4,3},{5,4},{6,5},{7,6},{8,7},{9,8},{10,9... | collective-permute-start | bytes 147464 | tf_op jit(solution)/shard_map/ppermute | solution.py:13
  (27 other events, 294.8 us)
